TPU v7x, 32 devices: a whole 2x2x4 slice. The times are simulated.
32 devices in a mesh: node: 8 (over z, x), mp: 4 (over y, core).
Axes of the slice: x: 2, y: 2, z: 4, core: 2. Of those that a mesh axis runs over, the one named last changes fastest.
Arguments:
- stored_features: float32 [16384, 1024], P('node', 'mp'), may hold values from -6 to 6
- vertex_row_index: int32 [16384], P('node'), may hold values from 0 to 511
- neighbors: int32 [2, 16384, 16], P(None, 'node'), may hold values from 0 to 511
- counts: int32 [2, 16384], P(None, 'node'), may hold values from 1 to 16
- self_w1: float32 [1024, 256], P('mp'), may hold values from -0.1875 to 0.1875
- neigh_w1: float32 [1024, 256], P('mp'), may hold values from -0.1875 to 0.1875
- self_w2: float32 [256, 256], replicated, may hold values from -0.375 to 0.375
- neigh_w2: float32 [256, 256], replicated, may hold values from -0.375 to 0.375
- upstream: float32 [32, 512, 256], P('node', 'mp'), may hold values from -6 to 6
Outputs:
- layer_out: float32 [32, 512, 256], P('node', 'mp')
- grad_self1: float32 [1024, 256], P('mp')
- grad_neigh1: float32 [1024, 256], P('mp')
- grad_self2: float32 [256, 256], replicated
- grad_neigh2: float32 [256, 256], replicated
Inputs may be any that keep to these rules, and one draw needn't show every extreme that they name: Only the first counts[l, r] slots of neighbors[l, r] are used; neighbour and stored-row numbers refer to the node's own subgraph.
All inputs are finite; a program needn't handle non-finite values.
Results may differ from a plain program's by a relative error of at most 0.003.
Values sent between devices are 32-bit elements; how exact they have to be, the bound alone decides.
A program may use at most 64 MiB of HBM per device.

v0:
```python
import math

import jax
import jax.numpy as jnp
from jax import lax
from jax.sharding import PartitionSpec as P

epsilon = 1e-05
precise = lax.Precision.HIGHEST


def adjacency(neighbor_ids, row_counts, width):
    row_total = neighbor_ids.shape[0]
    slot_positions = neighbor_ids.shape[1]
    tile_rows = min(128, row_total)
    tiles = row_total // tile_rows
    column_ids = jnp.arange(width, dtype=jnp.int32)
    slot_ids = jnp.arange(slot_positions, dtype=jnp.int32)
    slot_weight = (slot_ids[None, :] < row_counts[:, None]).astype(jnp.float32) / row_counts[
        :, None
    ].astype(jnp.float32)

    def one_tile(packed):
        tile_ids, tile_weight = packed
        hits = (tile_ids[:, :, None] == column_ids[None, None, :]).astype(jnp.float32)
        return jnp.sum(hits * tile_weight[:, :, None], axis=1)

    tiled = lax.map(
        one_tile,
        (
            neighbor_ids.reshape(tiles, tile_rows, slot_positions),
            slot_weight.reshape(tiles, tile_rows, slot_positions),
        ),
    )
    return tiled.reshape(row_total, width)


def normed_parts(pre_act):
    activated = jnp.maximum(pre_act, 0.0)
    inverse = lax.rsqrt(jnp.mean(activated * activated, axis=1, keepdims=True) + epsilon)
    return (activated * inverse, activated, inverse)


def norm_backward(hidden_grad, activated, inverse, pre_act):
    inner_sum = jnp.mean(hidden_grad * activated, axis=1, keepdims=True)
    act_grad = inverse * hidden_grad - activated * (inverse * inverse * inverse) * inner_sum
    return jnp.where(pre_act > 0, act_grad, 0.0)


def body(
    stored_features,
    vertex_row_index,
    neighbors,
    counts,
    self_w1,
    neigh_w1,
    self_w2,
    neigh_w2,
    upstream,
):
    mp_index = lax.axis_index("mp")
    sampled_graphs = upstream.shape[0]
    own_rows = upstream.shape[1]
    row_grand_total = vertex_row_index.shape[0] // sampled_graphs
    column_total = stored_features.shape[1]
    slot_positions = neighbors.shape[2]
    gradient_scale = 1.0 / math.sqrt(row_grand_total * sampled_graphs * lax.axis_size("node"))
    first_row = mp_index * own_rows
    stored_blocks = stored_features.reshape(sampled_graphs, row_grand_total, column_total)
    vertex_blocks = vertex_row_index.reshape(sampled_graphs, row_grand_total)
    neighbor_blocks = jnp.transpose(
        neighbors.reshape(2, sampled_graphs, row_grand_total, slot_positions), (1, 0, 2, 3)
    )
    block_count = jnp.transpose(counts.reshape(2, sampled_graphs, row_grand_total), (1, 0, 2))

    def one_graph(carry, packed):
        store_rows, node_rows, neighbor_ids, row_counts, cotangent = packed
        features = jnp.take(store_rows, node_rows, axis=0)
        adj_zero = adjacency(neighbor_ids[0], row_counts[0], row_grand_total)
        agg_zero = jnp.dot(adj_zero, features, precision=precise)
        own_ids = lax.dynamic_slice_in_dim(neighbor_ids[1], first_row, own_rows, 0)
        own_counts = lax.dynamic_slice_in_dim(row_counts[1], first_row, own_rows, 0)
        adj_own = adjacency(own_ids, own_counts, row_grand_total)
        scaled = cotangent * gradient_scale
        back_neigh = jnp.dot(scaled, neigh_w2.T, precision=precise)
        back_self = jnp.dot(scaled, self_w2.T, precision=precise)
        contrib = lax.dot_general(adj_own, back_neigh, (((0,), (0,)), ((), ())), precision=precise)
        rows_self = features
        rows_neigh = agg_zero
        pre_own = lax.psum_scatter(
            jnp.dot(rows_self, self_w1, precision=precise)
            + jnp.dot(rows_neigh, neigh_w1, precision=precise),
            "mp",
            scatter_dimension=0,
            tiled=True,
        )
        hidden_own, act_own, inverse_own = normed_parts(pre_own)
        hidden_all = lax.all_gather(hidden_own, "mp", axis=0, tiled=True)
        agg_one = jnp.dot(adj_own, hidden_all, precision=precise)
        hidden_grad = lax.psum_scatter(contrib, "mp", scatter_dimension=0, tiled=True) + back_self
        pre_grad = norm_backward(hidden_grad, act_own, inverse_own, pre_own)
        grad_piece = lax.all_gather(pre_grad, "mp", axis=0, tiled=True)
        rows_self = features
        rows_neigh = agg_zero
        step_self1 = carry[0] + jnp.dot(rows_self.T, grad_piece, precision=precise)
        step_neigh1 = carry[1] + jnp.dot(rows_neigh.T, grad_piece, precision=precise)
        graph_out = jnp.dot(hidden_own, self_w2, precision=precise) + jnp.dot(
            agg_one, neigh_w2, precision=precise
        )
        step_self2 = carry[2] + jnp.dot(hidden_own.T, scaled, precision=precise)
        step_neigh2 = carry[3] + jnp.dot(agg_one.T, scaled, precision=precise)
        return ((step_self1, step_neigh1, step_self2, step_neigh2), graph_out)

    zero_first = jnp.zeros(self_w1.shape, jnp.float32)
    zero_second = jnp.zeros(self_w2.shape, jnp.float32)
    totals, layer_out = lax.scan(
        one_graph,
        (zero_first, zero_first, zero_second, zero_second),
        (stored_blocks, vertex_blocks, neighbor_blocks, block_count, upstream),
    )
    grad_self1, grad_neigh1, grad_self2, grad_neigh2 = totals
    grad_self1, grad_neigh1, grad_self2, grad_neigh2 = lax.psum(
        (grad_self1, grad_neigh1, grad_self2, grad_neigh2), "node"
    )
    grad_self2, grad_neigh2 = lax.psum((grad_self2, grad_neigh2), "mp")
    return (layer_out, grad_self1, grad_neigh1, grad_self2, grad_neigh2)


def solution(mesh):
    placed = (
        P("node", "mp"),
        P("node"),
        P(None, "node", None),
        P(None, "node"),
        P("mp", None),
        P("mp", None),
        P(),
        P(),
        P("node", "mp", None),
    )
    return jax.shard_map(
        body,
        mesh=mesh,
        in_specs=placed,
        out_specs=(P("node", "mp", None), P("mp", None), P("mp", None), P(), P()),
        check_vma=False,
    )
```

profile of v0, /device:TPU:0, one launch (start us, length us, event | category | flops | bytes accessed | tf_op | source)
XLA Modules:
  0.0 468.3 jit_solution(11862067778070813773)
XLA Ops:
  8.1 1.8 reshape.157
  10.6 324.9 %while.44 = (s32[]{:T(128)}, f32[256,256]{1,0:T(8,128)S(1)}, f32[256,256]{1,0:T(8,128)S(1)}, f32[256,256]{1,0:T(8,128)S(1)}, f32[256,256]{1,0:T(8,128)S(1)}, /*i...) while((s32[]{:T(128)}, f32[256,256]{1,0:T(8,128)S(1)}, ...), condition=%wide.region_9.10_spmd.clone, body=%wide.region_0.9_spmd.clone.sunk | while | flops 3430420992 | bytes 29784160 | solution.py:116
  12.2 5.4 %while.45 = (s32[]{:T(128)}, f32[4,128,512]{2,1,0:T(8,128)S(1)}, s32[4,128,16]{1,0,2:T(4,128)S(1)}, f32[4,128,16]{1,2,0:T(8,128)S(1)}, s32[]{:T(128)}) while((s32[]{:T(128)}, f32[4,128,512]{2,1,0:T(8,128)S(1)}, s32[4,128,16]{1,0,2:T(4,128)S(1)}, f32[4,128,16]{1,2,0:T(8,128)S(1)}, s32[]{:T(128)}) %tuple.95), condition=%wide.region_3.3_spmd.clone, body=%wide.region_1.2_spmd.clone.sunk | while | flops 3080194 | bytes 868425 | solution.py:28
  12.5 1.1 select_reduce_fusion.5
  15.2 1.1 select_reduce_fusion.5
  17.7 1.1 dynamic-slice_bitcast_fusion.6
  18.8 1.6 gather_fusion
  20.4 1.1 fusion.117
  22.1 1.4 convolution_add_fusion.12
  25.4 1.1 select_reduce_fusion.4
  26.9 1.4 fusion.120
  28.4 19.7 %reduce-scatter.3.cloned.1.call-done = f32[128,256]{1,0:T(8,128)} async-done(((f32[512,256]{1,0:T(8,128)}), f32[128,256]{1,0:T(8,128)}) %reduce-scatter.3.cloned.1.call-update) | async-done | bytes 131088 | tf_op jit(solution)/shard_map/while/body/eval_jaxpr/reduce_scatter | solution.py:90
  48.1 24.2 %reduce-scatter.5.cloned.1.call-done = f32[128,256]{1,0:T(8,128)} async-done(((f32[512,256]{1,0:T(8,128)}), f32[128,256]{1,0:T(8,128)}) %reduce-scatter.5.cloned.1.call-update) | async-done | bytes 131088 | tf_op jit(solution)/shard_map/while/body/eval_jaxpr/reduce_scatter | solution.py:100
  72.2 1.4 multiply_reduce_fusion.3
  74.7 6.6 %all_gather.15 = f32[512,256]{1,0:T(8,128)S(1)} all-gather(f32[128,256]{1,0:T(8,128)S(1)} %get-tuple-element.571), channel_id=1, replica_groups=mesh['node'=8,'mp'=4] {'mp'}, dimensions={0}, use_global_device_ids=true | all-gather | bytes 655360 | tf_op jit(solution)/shard_map/while/body/eval_jaxpr/all_gather | solution.py:98
  82.0 7.3 %all_gather.14 = f32[512,256]{1,0:T(8,128)S(1)} all-gather(f32[128,256]{1,0:T(8,128)S(1)} %get-tuple-element.570), channel_id=1, replica_groups=mesh['node'=8,'mp'=4] {'mp'}, dimensions={0}, use_global_device_ids=true | all-gather | bytes 655360 | tf_op jit(solution)/shard_map/while/body/eval_jaxpr/all_gather | solution.py:102
  90.3 1.1 convolution_add_fusion.13
  95.1 5.4 %while.45 = (s32[]{:T(128)}, f32[4,128,512]{2,1,0:T(8,128)S(1)}, s32[4,128,16]{1,0,2:T(4,128)S(1)}, f32[4,128,16]{1,2,0:T(8,128)S(1)}, s32[]{:T(128)}) while((s32[]{:T(128)}, f32[4,128,512]{2,1,0:T(8,128)S(1)}, s32[4,128,16]{1,0,2:T(4,128)S(1)}, f32[4,128,16]{1,2,0:T(8,128)S(1)}, s32[]{:T(128)}) %tuple.95), condition=%wide.region_3.3_spmd.clone, body=%wide.region_1.2_spmd.clone.sunk | while | flops 3080194 | bytes 868425 | solution.py:28
  96.7 1.1 select_reduce_fusion.5
  99.4 1.1 select_reduce_fusion.5
  100.6 1.1 dynamic-slice_bitcast_fusion.6
  101.7 1.6 gather_fusion
  103.3 1.1 fusion.117
  105.0 1.4 convolution_add_fusion.12
  108.3 1.1 select_reduce_fusion.4
  109.8 1.4 fusion.120
  111.3 17.6 %reduce-scatter.3.cloned.1.call-done = f32[128,256]{1,0:T(8,128)} async-done(((f32[512,256]{1,0:T(8,128)}), f32[128,256]{1,0:T(8,128)}) %reduce-scatter.3.cloned.1.call-update) | async-done | bytes 131088 | tf_op jit(solution)/shard_map/while/body/eval_jaxpr/reduce_scatter | solution.py:90
  128.8 24.1 %reduce-scatter.5.cloned.1.call-done = f32[128,256]{1,0:T(8,128)} async-done(((f32[512,256]{1,0:T(8,128)}), f32[128,256]{1,0:T(8,128)}) %reduce-scatter.5.cloned.1.call-update) | async-done | bytes 131088 | tf_op jit(solution)/shard_map/while/body/eval_jaxpr/reduce_scatter | solution.py:100
  152.9 1.4 multiply_reduce_fusion.3
  155.4 6.6 %all_gather.15 = f32[512,256]{1,0:T(8,128)S(1)} all-gather(f32[128,256]{1,0:T(8,128)S(1)} %get-tuple-element.571), channel_id=1, replica_groups=mesh['node'=8,'mp'=4] {'mp'}, dimensions={0}, use_global_device_ids=true | all-gather | bytes 655360 | tf_op jit(solution)/shard_map/while/body/eval_jaxpr/all_gather | solution.py:98
  162.7 7.3 %all_gather.14 = f32[512,256]{1,0:T(8,128)S(1)} all-gather(f32[128,256]{1,0:T(8,128)S(1)} %get-tuple-element.570), channel_id=1, replica_groups=mesh['node'=8,'mp'=4] {'mp'}, dimensions={0}, use_global_device_ids=true | all-gather | bytes 655360 | tf_op jit(solution)/shard_map/while/body/eval_jaxpr/all_gather | solution.py:102
  171.0 1.1 convolution_add_fusion.13
  175.8 5.4 %while.45 = (s32[]{:T(128)}, f32[4,128,512]{2,1,0:T(8,128)S(1)}, s32[4,128,16]{1,0,2:T(4,128)S(1)}, f32[4,128,16]{1,2,0:T(8,128)S(1)}, s32[]{:T(128)}) while((s32[]{:T(128)}, f32[4,128,512]{2,1,0:T(8,128)S(1)}, s32[4,128,16]{1,0,2:T(4,128)S(1)}, f32[4,128,16]{1,2,0:T(8,128)S(1)}, s32[]{:T(128)}) %tuple.95), condition=%wide.region_3.3_spmd.clone, body=%wide.region_1.2_spmd.clone.sunk | while | flops 3080194 | bytes 868425 | solution.py:28
  181.2 1.1 dynamic-slice_bitcast_fusion.6
  182.3 1.6 gather_fusion
  183.9 1.1 fusion.117
  185.7 1.4 convolution_add_fusion.12
  189.0 1.1 select_reduce_fusion.4
  190.5 1.4 fusion.120
  191.9 17.5 %reduce-scatter.3.cloned.1.call-done = f32[128,256]{1,0:T(8,128)} async-done(((f32[512,256]{1,0:T(8,128)}), f32[128,256]{1,0:T(8,128)}) %reduce-scatter.3.cloned.1.call-update) | async-done | bytes 131088 | tf_op jit(solution)/shard_map/while/body/eval_jaxpr/reduce_scatter | solution.py:90
  209.5 24.0 %reduce-scatter.5.cloned.1.call-done = f32[128,256]{1,0:T(8,128)} async-done(((f32[512,256]{1,0:T(8,128)}), f32[128,256]{1,0:T(8,128)}) %reduce-scatter.5.cloned.1.call-update) | async-done | bytes 131088 | tf_op jit(solution)/shard_map/while/body/eval_jaxpr/reduce_scatter | solution.py:100
  233.5 1.4 multiply_reduce_fusion.3
  236.0 6.6 %all_gather.15 = f32[512,256]{1,0:T(8,128)S(1)} all-gather(f32[128,256]{1,0:T(8,128)S(1)} %get-tuple-element.571), channel_id=1, replica_groups=mesh['node'=8,'mp'=4] {'mp'}, dimensions={0}, use_global_device_ids=true | all-gather | bytes 655360 | tf_op jit(solution)/shard_map/while/body/eval_jaxpr/all_gather | solution.py:98
  243.3 7.3 %all_gather.14 = f32[512,256]{1,0:T(8,128)S(1)} all-gather(f32[128,256]{1,0:T(8,128)S(1)} %get-tuple-element.570), channel_id=1, replica_groups=mesh['node'=8,'mp'=4] {'mp'}, dimensions={0}, use_global_device_ids=true | all-gather | bytes 655360 | tf_op jit(solution)/shard_map/while/body/eval_jaxpr/all_gather | solution.py:102
  251.6 1.1 convolution_add_fusion.13
  256.4 5.4 %while.45 = (s32[]{:T(128)}, f32[4,128,512]{2,1,0:T(8,128)S(1)}, s32[4,128,16]{1,0,2:T(4,128)S(1)}, f32[4,128,16]{1,2,0:T(8,128)S(1)}, s32[]{:T(128)}) while((s32[]{:T(128)}, f32[4,128,512]{2,1,0:T(8,128)S(1)}, s32[4,128,16]{1,0,2:T(4,128)S(1)}, f32[4,128,16]{1,2,0:T(8,128)S(1)}, s32[]{:T(128)}) %tuple.95), condition=%wide.region_3.3_spmd.clone, body=%wide.region_1.2_spmd.clone.sunk | while | flops 3080194 | bytes 868425 | solution.py:28
  261.8 1.1 dynamic-slice_bitcast_fusion.6
  262.9 1.6 gather_fusion
  264.5 1.1 fusion.117
  266.3 1.4 convolution_add_fusion.12
  269.6 1.1 select_reduce_fusion.4
  271.1 1.4 fusion.120
  272.5 17.5 %reduce-scatter.3.cloned.1.call-done = f32[128,256]{1,0:T(8,128)} async-done(((f32[512,256]{1,0:T(8,128)}), f32[128,256]{1,0:T(8,128)}) %reduce-scatter.3.cloned.1.call-update) | async-done | bytes 131088 | tf_op jit(solution)/shard_map/while/body/eval_jaxpr/reduce_scatter | solution.py:90
  290.1 24.2 %reduce-scatter.5.cloned.1.call-done = f32[128,256]{1,0:T(8,128)} async-done(((f32[512,256]{1,0:T(8,128)}), f32[128,256]{1,0:T(8,128)}) %reduce-scatter.5.cloned.1.call-update) | async-done | bytes 131088 | tf_op jit(solution)/shard_map/while/body/eval_jaxpr/reduce_scatter | solution.py:100
  314.3 1.4 multiply_reduce_fusion.3
  316.8 6.6 %all_gather.15 = f32[512,256]{1,0:T(8,128)S(1)} all-gather(f32[128,256]{1,0:T(8,128)S(1)} %get-tuple-element.571), channel_id=1, replica_groups=mesh['node'=8,'mp'=4] {'mp'}, dimensions={0}, use_global_device_ids=true | all-gather | bytes 655360 | tf_op jit(solution)/shard_map/while/body/eval_jaxpr/all_gather | solution.py:98
  324.1 7.3 %all_gather.14 = f32[512,256]{1,0:T(8,128)S(1)} all-gather(f32[128,256]{1,0:T(8,128)S(1)} %get-tuple-element.570), channel_id=1, replica_groups=mesh['node'=8,'mp'=4] {'mp'}, dimensions={0}, use_global_device_ids=true | all-gather | bytes 655360 | tf_op jit(solution)/shard_map/while/body/eval_jaxpr/all_gather | solution.py:102
  332.4 1.1 convolution_add_fusion.13
  336.6 82.6 %all-reduce.5.cloned.1.call-done = (f32[256,256]{1,0:T(8,128)}, f32[256,256]{1,0:T(8,128)}, f32[256,256]{1,0:T(8,128)}, f32[256,256]{1,0:T(8,128)}) async-done(((f32[256,256]{1,0:T(8,128)}, f32[256,256]{1,0:T(8,128)}, f32[256,256]{1,0:T(8,128)}, f32[256,256]{1,0:T(8,128)}), (f32[256,256]{1,0:T(8,128)}, f32[256,256]{1,0:T(8,128)}, f32[256,256]{1,0:T(8,128)}, ...) | async-done | bytes 1048592 | tf_op jit(solution)/shard_map/psum | solution.py:122
  419.1 35.1 %all-reduce.7.cloned.1.call-done = (f32[256,256]{1,0:T(8,128)}, f32[256,256]{1,0:T(8,128)}) async-done(((f32[256,256]{1,0:T(8,128)}, f32[256,256]{1,0:T(8,128)}), (f32[256,256]{1,0:T(8,128)}, f32[256,256]{1,0:T(8,128)})) %all-reduce.7.cloned.1.call-update) | async-done | bytes 524304 | tf_op jit(solution)/shard_map/psum | solution.py:125
  454.2 1.7 copy.75
  455.9 1.7 copy.76
  457.6 1.7 copy.77
  459.2 1.7 copy.78
  (258 shorter events, 55.7 us)
Async XLA Ops:
  10.6 37.5 %reduce-scatter.3.cloned.1.call-start = ((), (), s32[]{:S(2)}) async-start(), calls=%async_computation.4 | async-start | bytes 655360 | tf_op jit(solution)/shard_map/while/body/eval_jaxpr/reduce_scatter | solution.py:90
  20.3 1.1 copy-start.7
  20.3 1.8 copy-start.8
  21.5 5.0 %copy-start = (f32[256,256]{1,0:T(8,128)S(1)}, f32[256,256]{1,0:T(8,128)}, u32[]{:S(2)}) copy-start(f32[256,256]{1,0:T(8,128)} %get-tuple-element.646) | copy-start | bytes 786436 | tf_op jit(solution)/shard_map/while
  21.5 5.0 %copy-start.2 = (f32[4,128,256]{2,1,0:T(8,128)S(1)}, f32[4,128,256]{2,1,0:T(8,128)}, u32[]{:S(2)}) copy-start(f32[4,128,256]{2,1,0:T(8,128)} %get-tuple-element.645) | copy-start | bytes 1572868 | tf_op jit(solution)/shard_map/while
  22.1 50.1 %copy-start.1 = (f32[256,256]{1,0:T(8,128)S(1)}, f32[256,256]{1,0:T(8,128)}, u32[]{:S(2)}) copy-start(f32[256,256]{1,0:T(8,128)} %get-tuple-element.647) | copy-start | bytes 786436 | tf_op jit(solution)/shard_map/while
  23.5 48.7 %reduce-scatter.5.cloned.1.call-start = ((), (), s32[]{:S(2)}) async-start(), calls=%async_computation.5 | async-start | bytes 655360 | tf_op jit(solution)/shard_map/while/body/eval_jaxpr/reduce_scatter | solution.py:100
  93.5 35.3 %reduce-scatter.3.cloned.1.call-start = ((), (), s32[]{:S(2)}) async-start(), calls=%async_computation.4 | async-start | bytes 655360 | tf_op jit(solution)/shard_map/while/body/eval_jaxpr/reduce_scatter | solution.py:90
  103.2 1.1 copy-start.7
  103.2 1.8 copy-start.8
  104.4 5.0 %copy-start = (f32[256,256]{1,0:T(8,128)S(1)}, f32[256,256]{1,0:T(8,128)}, u32[]{:S(2)}) copy-start(f32[256,256]{1,0:T(8,128)} %get-tuple-element.646) | copy-start | bytes 786436 | tf_op jit(solution)/shard_map/while
  104.4 5.0 %copy-start.2 = (f32[4,128,256]{2,1,0:T(8,128)S(1)}, f32[4,128,256]{2,1,0:T(8,128)}, u32[]{:S(2)}) copy-start(f32[4,128,256]{2,1,0:T(8,128)} %get-tuple-element.645) | copy-start | bytes 1572868 | tf_op jit(solution)/shard_map/while
  105.0 47.9 %copy-start.1 = (f32[256,256]{1,0:T(8,128)S(1)}, f32[256,256]{1,0:T(8,128)}, u32[]{:S(2)}) copy-start(f32[256,256]{1,0:T(8,128)} %get-tuple-element.647) | copy-start | bytes 786436 | tf_op jit(solution)/shard_map/while
  106.4 46.5 %reduce-scatter.5.cloned.1.call-start = ((), (), s32[]{:S(2)}) async-start(), calls=%async_computation.5 | async-start | bytes 655360 | tf_op jit(solution)/shard_map/while/body/eval_jaxpr/reduce_scatter | solution.py:100
  174.2 35.3 %reduce-scatter.3.cloned.1.call-start = ((), (), s32[]{:S(2)}) async-start(), calls=%async_computation.4 | async-start | bytes 655360 | tf_op jit(solution)/shard_map/while/body/eval_jaxpr/reduce_scatter | solution.py:90
  183.9 1.1 copy-start.7
  183.9 1.8 copy-start.8
  185.0 5.0 %copy-start = (f32[256,256]{1,0:T(8,128)S(1)}, f32[256,256]{1,0:T(8,128)}, u32[]{:S(2)}) copy-start(f32[256,256]{1,0:T(8,128)} %get-tuple-element.646) | copy-start | bytes 786436 | tf_op jit(solution)/shard_map/while
  185.0 5.0 %copy-start.2 = (f32[4,128,256]{2,1,0:T(8,128)S(1)}, f32[4,128,256]{2,1,0:T(8,128)}, u32[]{:S(2)}) copy-start(f32[4,128,256]{2,1,0:T(8,128)} %get-tuple-element.645) | copy-start | bytes 1572868 | tf_op jit(solution)/shard_map/while
  185.7 47.8 %copy-start.1 = (f32[256,256]{1,0:T(8,128)S(1)}, f32[256,256]{1,0:T(8,128)}, u32[]{:S(2)}) copy-start(f32[256,256]{1,0:T(8,128)} %get-tuple-element.647) | copy-start | bytes 786436 | tf_op jit(solution)/shard_map/while
  187.1 46.4 %reduce-scatter.5.cloned.1.call-start = ((), (), s32[]{:S(2)}) async-start(), calls=%async_computation.5 | async-start | bytes 655360 | tf_op jit(solution)/shard_map/while/body/eval_jaxpr/reduce_scatter | solution.py:100
  254.8 35.3 %reduce-scatter.3.cloned.1.call-start = ((), (), s32[]{:S(2)}) async-start(), calls=%async_computation.4 | async-start | bytes 655360 | tf_op jit(solution)/shard_map/while/body/eval_jaxpr/reduce_scatter | solution.py:90
  264.5 1.1 copy-start.7
  264.5 1.8 copy-start.8
  265.6 5.0 %copy-start = (f32[256,256]{1,0:T(8,128)S(1)}, f32[256,256]{1,0:T(8,128)}, u32[]{:S(2)}) copy-start(f32[256,256]{1,0:T(8,128)} %get-tuple-element.646) | copy-start | bytes 786436 | tf_op jit(solution)/shard_map/while
  265.6 5.0 %copy-start.2 = (f32[4,128,256]{2,1,0:T(8,128)S(1)}, f32[4,128,256]{2,1,0:T(8,128)}, u32[]{:S(2)}) copy-start(f32[4,128,256]{2,1,0:T(8,128)} %get-tuple-element.645) | copy-start | bytes 1572868 | tf_op jit(solution)/shard_map/while
  266.3 48.0 %copy-start.1 = (f32[256,256]{1,0:T(8,128)S(1)}, f32[256,256]{1,0:T(8,128)}, u32[]{:S(2)}) copy-start(f32[256,256]{1,0:T(8,128)} %get-tuple-element.647) | copy-start | bytes 786436 | tf_op jit(solution)/shard_map/while
  267.7 46.5 %reduce-scatter.5.cloned.1.call-start = ((), (), s32[]{:S(2)}) async-start(), calls=%async_computation.5 | async-start | bytes 655360 | tf_op jit(solution)/shard_map/while/body/eval_jaxpr/reduce_scatter | solution.py:100
  335.5 0.7 copy-start.3
  335.5 0.8 copy-start.4
  335.5 0.9 copy-start.5
  335.5 1.0 copy-start.6
  335.5 83.6 %all-reduce.5.cloned.1.call-start = ((), (), s32[]{:S(2)}) async-start(), calls=%async_computation.2 | async-start | bytes 2097152 | tf_op jit(solution)/shard_map/psum | solution.py:122
  336.5 117.7 %all-reduce.7.cloned.1.call-start = ((), (), s32[]{:S(2)}) async-start(), calls=%async_computation.3 | async-start | bytes 1048576 | tf_op jit(solution)/shard_map/psum | solution.py:125
Sparse Core Ops, SparseCore 0:
  23.7 24.3 reduce-scatter.2
  50.5 21.6 reduce-scatter.4
  106.6 22.2 reduce-scatter.2
  131.2 21.6 reduce-scatter.4
  187.2 22.1 reduce-scatter.2
  211.8 21.6 reduce-scatter.4
  267.8 22.2 reduce-scatter.2
  292.6 21.6 reduce-scatter.4
Sparse Core Ops, SparseCore 1:
  340.5 78.6 all-reduce.4
  421.4 32.7 all-reduce.6
where the time goes:
time: 470 us; the launch traced here: 468 us
  waiting for transfers between devices  287 us (61%)
  blocking collectives  55.5 us (12%)
  matrix products  44.7 us (10%)
  local copies, waits for them, and re-layouts  35.4 us (8%)
  other arithmetic  28.6 us (6%)
  between operations  15.5 us (3%)
    reduce_scatter x4, waiting for transfers between devices, one_graph(): lax.psum_scatter(contrib, 'mp', scatter_dimension=0, tiled=True) + back_self  96.4 us
    psum x1, waiting for transfers between devices, body(): lax.psum((grad_self1, grad_neigh1, grad_self2, grad_neigh2), 'node')  82.6 us
    reduce_scatter x4, waiting for transfers between devices, one_graph(): lax.psum_scatter(jnp.dot(rows_self, self_w1, precision=precise) + jnp.dot...  72.3 us
    psum x1, waiting for transfers between devices, body(): grad_self2, grad_neigh2 = lax.psum((grad_self2, grad_neigh2), 'mp')  35.1 us
    all_gather x4, blocking collectives, one_graph(): grad_piece = lax.all_gather(pre_grad, 'mp', axis=0, tiled=True)  29.1 us
    all_gather x4, blocking collectives, one_graph(): hidden_all = lax.all_gather(hidden_own, 'mp', axis=0, tiled=True)  26.4 us
    reduce_sum x20, other arithmetic, one_tile(): return jnp.sum(hits * tile_weight[:, :, None], axis=1)  21.1 us
  transfers between devices with their start and end apart: 10, of which 10 were waited for; matrix products, arithmetic and copies ran while one was open for 4% of the time, Pallas kernels for 0%

commit v1 on v0

--- a/solution.py
+++ b/solution.py
@@ -1,8 +1,11 @@
+import functools
 import math
 
 import jax
 import jax.numpy as jnp
 from jax import lax
+from jax.experimental import pallas as pl
+from jax.experimental.pallas import tpu as pltpu
 from jax.sharding import PartitionSpec as P
 
 epsilon = 1e-05
@@ -126,6 +129,430 @@
     return (layer_out, grad_self1, grad_neigh1, grad_self2, grad_neigh2)
 
 
+f32 = jnp.float32
+bf16 = jnp.bfloat16
+
+
+def halves(value):
+    high = value.astype(bf16)
+    return high, (value - high.astype(f32)).astype(bf16)
+
+
+def thirds(value):
+    high = value.astype(bf16)
+    rest = value - high.astype(f32)
+    middle = rest.astype(bf16)
+    return high, middle, (rest - middle.astype(f32)).astype(bf16)
+
+
+def mul(left, right, dims=((1,), (0,))):
+    return lax.dot_general(left, right, (dims, ((), ())), preferred_element_type=f32)
+
+
+def mul3(left, right, dims=((1,), (0,))):
+    return (
+        mul(left[0], right[0], dims) + mul(left[1], right[0], dims) + mul(left[0], right[1], dims)
+    )
+
+
+def mul6(left, right):
+    small = mul(left[2], right[0]) + mul(left[0], right[2]) + mul(left[1], right[1])
+    return mul(left[0], right[0]) + (mul(left[0], right[1]) + mul(left[1], right[0]) + small)
+
+
+def fused_kernel(
+    node_total,
+    slots,
+    scale,
+    store_ref,
+    ids_ref,
+    w1_ref,
+    w2_ref,
+    up_ref,
+    out_ref,
+    g1_ref,
+    g2_ref,
+    upg,
+    part,
+    pin,
+    far,
+    pg,
+    xh,
+    xl,
+    xt,
+    wh,
+    wl,
+    wt,
+    onehot,
+    adj,
+    act_buf,
+    g1acc,
+    g2acc,
+    g2in,
+    q2,
+    q2r,
+    outg,
+    g1x,
+    g1h,
+    g1z,
+    q2x,
+    q2h,
+    q2z,
+    send_sems,
+    recv_sems,
+):
+    rows = upg.shape[0]
+    own = up_ref.shape[1]
+    cols = store_ref.shape[1]
+    depth = node_total // 2
+    node = lax.axis_index("node")
+    member = lax.axis_index("mp")
+    zc, xc = node // 2, node % 2
+    yc, cc = member // 2, member % 2
+    partner = yc * 2 + (1 - cc)
+    across = (1 - yc) * 2 + cc
+    diagonal = (1 - yc) * 2 + (1 - cc)
+    peers = (partner, across, diagonal)
+    x_peer = zc * 2 + (1 - xc)
+    z_next = [((zc + d) % depth) for d in range(1, depth)]
+    z_prev = [((zc + depth - d) % depth) for d in range(1, depth)]
+
+    def target(node_id, member_id):
+        return dict(device_id=(node_id, member_id), device_id_type=pl.DeviceIdType.MESH)
+
+    counter = [0]
+
+    def copy(source, dest, node_id, member_id):
+        k = counter[0]
+        counter[0] += 1
+        return pltpu.make_async_remote_copy(
+            src_ref=source,
+            dst_ref=dest,
+            send_sem=send_sems.at[k],
+            recv_sem=recv_sems.at[k],
+            **target(node_id, member_id),
+        )
+
+    barrier = pltpu.get_barrier_semaphore()
+    for p in peers:
+        pl.semaphore_signal(barrier, inc=1, **target(node, p))
+    pl.semaphore_signal(barrier, inc=1, **target(x_peer, member))
+    for z in z_next:
+        pl.semaphore_signal(barrier, inc=1, **target(z * 2 + xc, member))
+    pl.semaphore_wait(barrier, 4 + depth - 1)
+
+    def block(index, size):
+        return pl.ds(pl.multiple_of(index * size, size), size)
+
+    up_copies = [copy(up_ref.at[p], upg.at[block(member, own)], node, p) for p in peers]
+    for one in up_copies:
+        one.start()
+    upg[block(member, own)] = up_ref[member]
+    wh[...], wl[...], wt[...] = thirds(w1_ref[...])
+
+    tile = 64
+    lanes = lax.broadcasted_iota(jnp.int32, (tile, rows), 1)
+
+    def hits(picked, first):
+        total = jnp.zeros((tile, rows), f32)
+        for k in range(first, first + slots):
+            total = total + jnp.where(picked[:, k : k + 1] == lanes, 1.0, 0.0)
+        return total.astype(bf16)
+
+    def build(graph, first, with_vertex):
+        @pl.loop(0, rows // tile)
+        def _(t):
+            at = pl.ds(pl.multiple_of(graph * rows + t * tile, tile), tile)
+            picked = ids_ref[at]
+            to = block(t, tile)
+            adj[to] = hits(picked, first)
+            if with_vertex:
+                v = 2 * slots
+                onehot[to] = jnp.where(picked[:, v : v + 1] == lanes, 1.0, 0.0).astype(bf16)
+
+    def reciprocal(graph, layer):
+        k = 2 * slots + 1 + layer
+        return 1.0 / ids_ref[block(graph, rows), k : k + 1].astype(f32)
+
+    to_partner_a = copy(part.at[0], pin.at[0], node, partner)
+    to_across = copy(part.at[1], far, node, across)
+    to_partner_b = copy(part.at[2], pin.at[1], node, partner)
+
+    @pl.loop(0, 4)
+    def _(s):
+        gy = yc + (1 - s // 2) * (1 - 2 * yc)
+        gc = cc + (1 - s % 2) * (1 - 2 * cc)
+        graph = gy * 2 + gc
+        build(graph, 0, True)
+        sh, sl, st = thirds(store_ref[block(graph, rows)])
+        fh = mul(onehot[...], sh).astype(bf16)
+        fl = mul(onehot[...], sl).astype(bf16)
+        ft = mul(onehot[...], st).astype(bf16)
+        xh[s, :, :cols] = fh
+        xl[s, :, :cols] = fl
+        xt[:, :cols] = ft
+        agg = (mul(adj[...], ft) + mul(adj[...], fl) + mul(adj[...], fh)) * reciprocal(graph, 0)
+        ah, al, at = thirds(agg)
+        xt[:, cols:] = at
+        xh[s, :, cols:] = ah
+        xl[s, :, cols:] = al
+        part[s] = mul6((xh[s], xl[s], xt[...]), (wh[...], wl[...], wt[...]))
+
+        @pl.when(s == 0)
+        def _():
+            to_partner_a.start()
+
+        @pl.when(s == 1)
+        def _():
+            to_partner_a.wait_recv()
+            part[1] = part[1] + pin[0]
+            to_across.start()
+
+        @pl.when(s == 2)
+        def _():
+            to_partner_b.start()
+
+    build(member, slots, False)
+    shrink = reciprocal(member, 1)
+    for one in up_copies:
+        one.wait_recv()
+    scaled = halves(upg[...] * scale)
+    w2s = halves(w2_ref[: w2_ref.shape[0] // 2])
+    w2n = halves(w2_ref[w2_ref.shape[0] // 2 :])
+    nt = ((1,), (1,))
+    tn = ((0,), (0,))
+    back = halves(mul3(scaled, w2n, nt) * shrink)
+    hidden_grad = mul3(scaled, w2s, nt) + mul(adj[...], back[0], tn) + mul(adj[...], back[1], tn)
+    act_buf[...] = hidden_grad
+    to_partner_b.wait_recv()
+    near = part[3] + pin[1]
+    to_across.wait_recv()
+    pre = near + far[...]
+    hidden, activated, inverse = normed_parts(pre)
+    pg[3] = norm_backward(act_buf[...], activated, inverse, pre)
+    pg_partner = copy(pg.at[3], pg.at[2], node, partner)
+    pg_across = copy(pg.at[3], pg.at[1], node, across)
+    pg_forward = copy(pg.at[1], pg.at[0], node, partner)
+    pg_across.start()
+    pg_partner.start()
+
+    hid = halves(hidden)
+    agg_one = halves((mul(adj[...], hid[0]) + mul(adj[...], hid[1])) * shrink)
+    width = hidden.shape[1]
+    scaled = halves(upg[...] * scale)
+    g2acc[:width] = mul3(hid, scaled, tn)
+    g2acc[width:] = mul3(agg_one, scaled, tn)
+    quarter = g2acc.shape[0] // 4
+    g2_copies = [
+        copy(g2acc.at[block(p, quarter)], g2in.at[d], node, p) for d, p in enumerate(peers)
+    ]
+    for one in g2_copies:
+        one.start()
+    w2s = halves(w2_ref[:width])
+    w2n = halves(w2_ref[width:])
+    outg[...] = mul3(hid, w2s) + mul3(agg_one, w2n)
+    out_copies = [copy(outg.at[block(p, own)], out_ref.at[member], node, p) for p in peers]
+    for one in out_copies:
+        one.start()
+    out_ref[member] = outg[block(member, own)]
+
+    g1acc[...] = jnp.zeros_like(g1acc)
+
+    @pl.loop(0, 4)
+    def _(t):
+        s = 3 - t
+
+        @pl.when(t == 1)
+        def _():
+            pg_partner.wait_recv()
+
+        @pl.when(t == 2)
+        def _():
+            pg_across.wait_recv()
+            pg_forward.start()
+
+        @pl.when(t == 3)
+        def _():
+            pg_forward.wait_recv()
+
+        g1acc[...] += mul3((xh[s], xl[s]), halves(pg[s]), tn)
+
+    sets = []
+    for full, x_in, half, z_in, result in (
+        (q2, q2x, q2h, q2z, q2r),
+        (g1acc, g1x, g1h, g1z, g1_ref),
+    ):
+        size = full.shape[0] // 2
+        piece = size // depth
+        x_copy = copy(full.at[block(1 - xc, size)], x_in, x_peer, member)
+        z_copies = [
+            copy(half.at[block(z, piece)], z_in.at[d], z * 2 + xc, member)
+            for d, z in enumerate(z_next)
+        ]
+        mine = pl.ds(pl.multiple_of(xc * size + zc * piece, piece), piece)
+        spread = [copy(result.at[mine], result.at[mine], z * 2 + xc, member) for z in z_next]
+        echo = [copy(result.at[mine], result.at[mine], x_peer, member)]
+        for z in z_prev:
+            there = pl.ds(pl.multiple_of(xc * size + z * piece, piece), piece)
+            echo.append(copy(result.at[there], result.at[there], x_peer, member))
+        sets.append((full, x_in, half, z_in, result, size, piece, x_copy, z_copies, mine, spread, echo))
+
+    def start_x(one):
+        one[7].start()
+
+    def start_z(one):
+        full, x_in, half, z_in, result, size, piece, x_copy, z_copies = one[:9]
+        x_copy.wait()
+        half[...] = full[block(xc, size)] + x_in[...]
+        for each in z_copies:
+            each.start()
+
+    def start_spread(one):
+        full, x_in, half, z_in, result, size, piece, x_copy, z_copies, mine, spread, echo = one
+        total = half[block(zc, piece)]
+        for d, each in enumerate(z_copies):
+            each.wait_recv()
+            total = total + z_in[d]
+        result[mine] = total
+        for each in spread:
+            each.start()
+        echo[0].start()
+
+    def relay(one):
+        spread, echo = one[10:]
+        for each, onward in zip(spread, echo[1:]):
+            each.wait_recv()
+            onward.start()
+
+    def finish(one):
+        z_copies, spread, echo = one[8], one[10], one[11]
+        for each in echo:
+            each.wait()
+        for each in z_copies + spread:
+            each.wait_send()
+
+    start_x(sets[1])
+    summed = g2acc[block(member, quarter)]
+    for d, one in enumerate(g2_copies):
+        one.wait_recv()
+        summed = summed + g2in[d]
+    q2[...] = summed
+    start_x(sets[0])
+    start_z(sets[1])
+    start_z(sets[0])
+    start_spread(sets[1])
+    start_spread(sets[0])
+    relay(sets[0])
+    relay(sets[1])
+    finish(sets[0])
+    here = block(member, quarter)
+    last = [copy(q2r, g2_ref.at[here], node, p) for p in peers]
+    for one in last:
+        one.start()
+    g2_ref[here] = q2r[...]
+    finish(sets[1])
+    for one in up_copies + [to_partner_a, to_across, to_partner_b, pg_partner, pg_across, pg_forward]:
+        one.wait_send()
+    for one in g2_copies:
+        one.wait_send()
+    for one in out_copies + last:
+        one.wait()
+
+
+def fused(mesh_node):
+    def run(stored, vertex, neighbors, counts, self_w1, neigh_w1, self_w2, neigh_w2, upstream):
+        graphs, own, width = upstream.shape
+        rows = vertex.shape[0] // graphs
+        slots = neighbors.shape[2]
+        cols = stored.shape[1]
+        total = vertex.shape[0]
+        used = lax.broadcasted_iota(jnp.int32, neighbors.shape, 2) < counts[:, :, None]
+        masked = jnp.where(used, neighbors, -1)
+        ids = jnp.concatenate(
+            [masked[0], masked[1], vertex[:, None], counts[0][:, None], counts[1][:, None]], axis=1
+        )
+        w1 = jnp.concatenate([self_w1, neigh_w1], axis=0)
+        w2 = jnp.concatenate([self_w2, neigh_w2], axis=0)
+        scale = 1.0 / math.sqrt(total * mesh_node)
+        depth = mesh_node // 2
+        wide = 2 * cols
+        quarter = 2 * width // 4
+        copies = 18 + 2 * (2 + 3 * (depth - 1))
+        vm = pltpu.VMEM
+        scratch = [
+            vm((rows, width), f32),
+            vm((4, rows, width), f32),
+            vm((2, rows, width), f32),
+            vm((rows, width), f32),
+            vm((4, rows, width), f32),
+            vm((4, rows, wide), bf16),
+            vm((4, rows, wide), bf16),
+            vm((rows, wide), bf16),
+            vm((wide, width), bf16),
+            vm((wide, width), bf16),
+            vm((wide, width), bf16),
+            vm((rows, rows), bf16),
+            vm((rows, rows), bf16),
+            vm((rows, width), f32),
+            vm((wide, width), f32),
+            vm((2 * width, width), f32),
+            vm((3, quarter, width), f32),
+            vm((quarter, width), f32),
+            vm((quarter, width), f32),
+            vm((rows, width), f32),
+            vm((wide // 2, width), f32),
+            vm((wide // 2, width), f32),
+            vm((depth - 1, wide // 2 // depth, width), f32),
+            vm((quarter // 2, width), f32),
+            vm((quarter // 2, width), f32),
+            vm((depth - 1, quarter // 2 // depth, width), f32),
+            pltpu.SemaphoreType.DMA((copies,)),
+            pltpu.SemaphoreType.DMA((copies,)),
+        ]
+        space = pl.BlockSpec(memory_space=pltpu.VMEM)
+        out, g1, g2 = pl.pallas_call(
+            functools.partial(fused_kernel, mesh_node, slots, scale),
+            out_shape=(
+                jax.ShapeDtypeStruct((graphs, own, width), f32),
+                jax.ShapeDtypeStruct((wide, width), f32),
+                jax.ShapeDtypeStruct((2 * width, width), f32),
+            ),
+            in_specs=[space] * 5,
+            out_specs=(space,) * 3,
+            scratch_shapes=scratch,
+            compiler_params=pltpu.CompilerParams(
+                collective_id=0, has_side_effects=True, vmem_limit_bytes=60 * 1024 * 1024
+            ),
+        )(stored, ids, w1, w2, upstream)
+        return out, g1[:cols], g1[cols:], g2[:width], g2[width:]
+
+    return run
+
+
+def fitted(mesh):
+    node_total, members = mesh.shape["node"], mesh.shape["mp"]
+
+    def run(*args):
+        vertex, upstream, stored = args[1], args[8], args[0]
+        graphs, own, width = upstream.shape
+        depth = node_total // 2
+        fits = (
+            members == 4
+            and graphs == members
+            and node_total % 2 == 0
+            and depth > 1
+            and own * members * graphs == vertex.shape[0]
+            and own % 64 == 0
+            and width % 128 == 0
+            and stored.shape[1] % 128 == 0
+            and (width // 4) % (8 * depth) == 0
+            and stored.shape[1] % (8 * depth) == 0
+        )
+        return (fused(node_total) if fits else body)(*args)
+
+    return run
+
+
 def solution(mesh):
     placed = (
         P("node", "mp"),
@@ -139,7 +566,7 @@
         P("node", "mp", None),
     )
     return jax.shard_map(
-        body,
+        fitted(mesh),
         mesh=mesh,
         in_specs=placed,
         out_specs=(P("node", "mp", None), P("mp", None), P("mp", None), P(), P()),

time: 470 us -> 95.9 us (0.20)
  waiting for transfers between devices: 287 us -> 0 us
  Pallas kernels: 0 us -> 85.2 us
  blocking collectives: 55.5 us -> 0 us
  matrix products: 44.7 us -> 0 us
  local copies, waits for them, and re-layouts: 35.4 us -> 5.96 us
  other arithmetic: 28.6 us -> 3.67 us
  between operations: 15.5 us -> 0.68 us
    reduce_scatter x8 -> x0, waiting for transfers between devices: 169 us -> none  [the longest x4 96.4 us: one_graph(): lax.psum_scatter(contrib, 'mp', scatter_dimension=0, tiled=True) + back_self]
    psum x2 -> x0, waiting for transfers between devices: 118 us -> none  [the longest x1 82.6 us: body(): lax.psum((grad_self1, grad_neigh1, grad_self2, grad_neigh2), 'node')]
    pallas_call x0 -> x1, Pallas kernels: none -> 85.2 us  [run(): pl.pallas_call(functools.partial(fused_kernel, mesh_node, slots, scale),...]
    all_gather x8 -> x0, blocking collectives: 55.5 us -> none  [the longest x4 29.1 us: one_graph(): grad_piece = lax.all_gather(pre_grad, 'mp', axis=0, tiled=True)]
    dot_general x52 -> x0, matrix products: 44.7 us -> none  [the longest x4 5.78 us: one_graph(): back_self = jnp.dot(scaled, self_w2.T, precision=precise)]
    reduce_sum x20 -> x0, other arithmetic: 21.1 us -> none  [one_tile(): return jnp.sum(hits * tile_weight[:, :, None], axis=1)]
    unnamed x12 -> x7, local copies, waits for them, and re-layouts: 7.58 us -> 0.81 us
    gather x4 -> x0, local copies, waits for them, and re-layouts: 6.29 us -> none  [one_graph(): features = jnp.take(store_rows, node_rows, axis=0)]
  transfers between devices with their start and end apart: 10 -> 0, of which waited for: 10 -> 0; matrix products, arithmetic and copies ran while one was open for 4% -> 0% of each run, Pallas kernels for 0% -> 0%
where the time goes in v1:
time: 95.9 us; the launch traced here: 95.5 us
  Pallas kernels  85.2 us (89%)
  local copies, waits for them, and re-layouts  5.96 us (6%)
  other arithmetic  3.67 us (4%)
    pallas_call x1, Pallas kernels, run(): pl.pallas_call(functools.partial(fused_kernel, mesh_node, slots, scale),...  85.2 us
    slice x1, local copies, waits for them, and re-layouts, run(): return (out, g1[:cols], g1[cols:], g2[:width], g2[width:])  2.23 us
    concatenate x2, local copies, waits for them, and re-layouts, run(): jnp.concatenate([masked[0], masked[1], vertex[:, None], counts[0][:, None...  2.1 us

profile of v1, /device:TPU:0, one launch (start us, length us, event | category | flops | bytes accessed | tf_op | source)
XLA Modules:
  0.0 95.5 jit_solution(4011608810228532936)
XLA Ops:
  0.6 0.0 copy-start.1
  0.6 0.0 copy-start.2
  0.7 0.8 slice_bitcast_fusion.2
  1.5 1.0 %fusion = s32[2,2048,16]{1,2,0:T(8,128)S(1)} fusion(s32[2,2048,16]{1,2,0:T(8,128)} %param.11, s32[2,2048]{1,0:T(2,128)} %param.12), kind=kLoop, calls=%fused_computation.3 | loop fusion | flops 131072 | bytes 540672 | tf_op jit(solution)/shard_map/jit(_where)/select_n | solution.py:470
  2.5 0.8 concatenate.9
  3.2 1.9 %pad_maximum_fusion.w1_ref = f32[512,256]{1,0:T(8,128)} fusion(f32[256,256]{1,0:T(8,128)} %param.14, f32[256,256]{1,0:T(8,128)} %param.13), kind=kLoop, calls=%fused_computation | loop fusion | flops 131072 | bytes 1048576 | tf_op jit(solution)/shard_map/concatenate | solution.py:474
  5.1 0.0 copy-done.1
  5.1 0.0 copy-done.2
  5.1 0.8 pad_maximum_fusion.1.w2_ref
  5.9 1.3 %copy.19.ids_ref = s32[2048,35]{1,0:T(8,128)} copy(s32[2048,35]{0,1:T(8,128)S(1)} %concatenate.9) | data formatting | bytes 573440 | tf_op jit(solution)/shard_map/concatenate | solution.py:471
  7.3 85.2 %shard_map.128 = (f32[4,128,256]{2,1,0:T(8,128)}, f32[512,256]{1,0:T(8,128)}, f32[512,256]{1,0:T(8,128)}) custom-call(f32[2048,256]{1,0:T(8,128)} %store_ref.1, s32[2048,35]{1,0:T(8,128)} %copy.19.ids_ref, f32[512,256]{1,0:T(8,128)} %pad_maximum_fusion.w1_ref, f32[512,256]{1,0:T(8,128)} %pad_maximum_fusion.1.w2_ref, f32[4,128,256]{2,1,0:T(8,128)} %up_ref.1), custom_call_target="tpu_custom_call" | custom-call | tf_op jit(solution)/shard_map/pallas_call | solution.py:513
  92.5 0.0 copy-start
  92.5 2.2 %fusion.1 = (f32[256,256]{1,0:T(8,128)}, f32[256,256]{1,0:T(8,128)}, f32[256,256]{1,0:T(8,128)}, f32[256,256]{1,0:T(8,128)}) fusion(f32[512,256]{1,0:T(8,128)} %get-tuple-element.10, f32[512,256]{1,0:T(8,128)} %get-tuple-element.9), kind=kLoop, calls=%fused_computation.8 | loop fusion | bytes 2097152 | tf_op jit(solution)/shard_map/slice | solution.py:527
  94.7 0.0 copy-done
  94.7 0.8 copy.21
  (1 shorter events, 0.0 us)
Async XLA Ops:
  0.6 4.5 %copy-start.1 = (f32[256,256]{1,0:T(8,128)S(1)}, f32[256,256]{1,0:T(8,128)}, u32[]{:S(2)}) copy-start(f32[256,256]{1,0:T(8,128)} %param.16) | copy-start | bytes 786436
  0.6 4.5 %copy-start.2 = (f32[256,256]{1,0:T(8,128)S(1)}, f32[256,256]{1,0:T(8,128)}, u32[]{:S(2)}) copy-start(f32[256,256]{1,0:T(8,128)} %param.15) | copy-start | bytes 786436
  92.5 2.2 %copy-start = (f32[4,128,256]{2,1,0:T(8,128)S(1)}, f32[4,128,256]{2,1,0:T(8,128)}, u32[]{:S(2)}) copy-start(f32[4,128,256]{2,1,0:T(8,128)} %get-tuple-element.26) | copy-start | bytes 1572868

commit v2 on v1

--- a/solution.py
+++ b/solution.py
@@ -166,8 +166,10 @@
     scale,
     store_ref,
     ids_ref,
-    w1_ref,
-    w2_ref,
+    s1_ref,
+    n1_ref,
+    s2_ref,
+    n2_ref,
     up_ref,
     out_ref,
     g1_ref,
@@ -192,12 +194,9 @@
     q2,
     q2r,
     outg,
-    g1x,
-    g1h,
-    g1z,
-    q2x,
-    q2h,
-    q2z,
+    xin,
+    xhalf,
+    zin,
     send_sems,
     recv_sems,
 ):
@@ -248,27 +247,30 @@
     for one in up_copies:
         one.start()
     upg[block(member, own)] = up_ref[member]
-    wh[...], wl[...], wt[...] = thirds(w1_ref[...])
+    wh[:cols], wl[:cols], wt[:cols] = thirds(s1_ref[...])
+    wh[cols:], wl[cols:], wt[cols:] = thirds(n1_ref[...])
 
     tile = 64
-    lanes = lax.broadcasted_iota(jnp.int32, (tile, rows), 1)
+    middle = rows // 2
+    lanes = (lax.broadcasted_iota(jnp.int32, (tile, rows), 1) - middle).astype(f32).astype(bf16)
+    one_b, none_b = jnp.ones((), bf16), jnp.zeros((), bf16)
 
     def hits(picked, first):
-        total = jnp.zeros((tile, rows), f32)
+        total = jnp.zeros((tile, rows), bf16)
         for k in range(first, first + slots):
-            total = total + jnp.where(picked[:, k : k + 1] == lanes, 1.0, 0.0)
-        return total.astype(bf16)
+            total = total + jnp.where(picked[:, k : k + 1] == lanes, one_b, none_b)
+        return total
 
     def build(graph, first, with_vertex):
         @pl.loop(0, rows // tile)
         def _(t):
             at = pl.ds(pl.multiple_of(graph * rows + t * tile, tile), tile)
-            picked = ids_ref[at]
+            picked = (ids_ref[at] - middle).astype(f32).astype(bf16)
             to = block(t, tile)
             adj[to] = hits(picked, first)
             if with_vertex:
                 v = 2 * slots
-                onehot[to] = jnp.where(picked[:, v : v + 1] == lanes, 1.0, 0.0).astype(bf16)
+                onehot[to] = jnp.where(picked[:, v : v + 1] == lanes, one_b, none_b)
 
     def reciprocal(graph, layer):
         k = 2 * slots + 1 + layer
@@ -317,8 +319,8 @@
     for one in up_copies:
         one.wait_recv()
     scaled = halves(upg[...] * scale)
-    w2s = halves(w2_ref[: w2_ref.shape[0] // 2])
-    w2n = halves(w2_ref[w2_ref.shape[0] // 2 :])
+    w2s = halves(s2_ref[...])
+    w2n = halves(n2_ref[...])
     nt = ((1,), (1,))
     tn = ((0,), (0,))
     back = halves(mul3(scaled, w2n, nt) * shrink)
@@ -331,9 +333,11 @@
     hidden, activated, inverse = normed_parts(pre)
     pg[3] = norm_backward(act_buf[...], activated, inverse, pre)
     pg_partner = copy(pg.at[3], pg.at[2], node, partner)
-    pg_across = copy(pg.at[3], pg.at[1], node, across)
-    pg_forward = copy(pg.at[1], pg.at[0], node, partner)
-    pg_across.start()
+    parts = [pl.ds(i * own, own) for i in range(4)]
+    pg_across = [copy(pg.at[3, r], pg.at[1, r], node, across) for r in parts]
+    pg_forward = [copy(pg.at[1, r], pg.at[0, r], node, partner) for r in parts]
+    for one in pg_across:
+        one.start()
     pg_partner.start()
 
     hid = halves(hidden)
@@ -348,8 +352,8 @@
     ]
     for one in g2_copies:
         one.start()
-    w2s = halves(w2_ref[:width])
-    w2n = halves(w2_ref[width:])
+    w2s = halves(s2_ref[...])
+    w2n = halves(n2_ref[...])
     outg[...] = mul3(hid, w2s) + mul3(agg_one, w2n)
     out_copies = [copy(outg.at[block(p, own)], out_ref.at[member], node, p) for p in peers]
     for one in out_copies:
@@ -368,90 +372,98 @@
 
         @pl.when(t == 2)
         def _():
-            pg_across.wait_recv()
-            pg_forward.start()
+            for one, onward in zip(pg_across, pg_forward):
+                one.wait_recv()
+                onward.start()
 
         @pl.when(t == 3)
         def _():
-            pg_forward.wait_recv()
+            for one in pg_forward:
+                one.wait_recv()
 
         g1acc[...] += mul3((xh[s], xl[s]), halves(pg[s]), tn)
 
     sets = []
-    for full, x_in, half, z_in, result in (
-        (q2, q2x, q2h, q2z, q2r),
-        (g1acc, g1x, g1h, g1z, g1_ref),
-    ):
-        size = full.shape[0] // 2
+    chunk = q2.shape[0]
+    pieces = g1acc.shape[0] // chunk
+    for full, base, i, result in [(g1acc, e * chunk, e, g1_ref) for e in range(pieces)] + [
+        (q2, 0, pieces, q2r)
+    ]:
+        size = chunk // 2
         piece = size // depth
-        x_copy = copy(full.at[block(1 - xc, size)], x_in, x_peer, member)
+        x_in, half, z_in = xin.at[i], xhalf.at[i], zin.at[i]
+        away = pl.ds(pl.multiple_of(base + (1 - xc) * size, size), size)
+        home = pl.ds(pl.multiple_of(base + xc * size, size), size)
+        x_copy = copy(full.at[away], x_in, x_peer, member)
         z_copies = [
-            copy(half.at[block(z, piece)], z_in.at[d], z * 2 + xc, member)
+            copy(xhalf.at[i, block(z, piece)], zin.at[i, d], z * 2 + xc, member)
             for d, z in enumerate(z_next)
         ]
-        mine = pl.ds(pl.multiple_of(xc * size + zc * piece, piece), piece)
+        mine = pl.ds(pl.multiple_of(base + xc * size + zc * piece, piece), piece)
         spread = [copy(result.at[mine], result.at[mine], z * 2 + xc, member) for z in z_next]
         echo = [copy(result.at[mine], result.at[mine], x_peer, member)]
         for z in z_prev:
-            there = pl.ds(pl.multiple_of(xc * size + z * piece, piece), piece)
+            there = pl.ds(pl.multiple_of(base + xc * size + z * piece, piece), piece)
             echo.append(copy(result.at[there], result.at[there], x_peer, member))
-        sets.append((full, x_in, half, z_in, result, size, piece, x_copy, z_copies, mine, spread, echo))
-
-    def start_x(one):
-        one[7].start()
+        sets.append((full, home, i, piece, result, x_copy, z_copies, mine, spread, echo))
 
     def start_z(one):
-        full, x_in, half, z_in, result, size, piece, x_copy, z_copies = one[:9]
+        full, home, i, piece, result, x_copy, z_copies = one[:7]
         x_copy.wait()
-        half[...] = full[block(xc, size)] + x_in[...]
+        xhalf[i] = full[home] + xin[i]
         for each in z_copies:
             each.start()
 
     def start_spread(one):
-        full, x_in, half, z_in, result, size, piece, x_copy, z_copies, mine, spread, echo = one
-        total = half[block(zc, piece)]
+        full, home, i, piece, result, x_copy, z_copies, mine, spread, echo = one
+        total = xhalf[i, block(zc, piece)]
         for d, each in enumerate(z_copies):
             each.wait_recv()
-            total = total + z_in[d]
+            total = total + zin[i, d]
         result[mine] = total
         for each in spread:
             each.start()
         echo[0].start()
 
     def relay(one):
-        spread, echo = one[10:]
-        for each, onward in zip(spread, echo[1:]):
+        for each, onward in zip(one[8], one[9][1:]):
             each.wait_recv()
             onward.start()
 
     def finish(one):
-        z_copies, spread, echo = one[8], one[10], one[11]
-        for each in echo:
+        for each in one[9]:
             each.wait()
-        for each in z_copies + spread:
+        for each in one[6] + one[8]:
             each.wait_send()
 
-    start_x(sets[1])
+    first, second = sets[:-1], sets[-1]
+    for one in first:
+        one[5].start()
+    for one in first[:-1]:
+        start_z(one)
     summed = g2acc[block(member, quarter)]
     for d, one in enumerate(g2_copies):
         one.wait_recv()
         summed = summed + g2in[d]
     q2[...] = summed
-    start_x(sets[0])
-    start_z(sets[1])
-    start_z(sets[0])
-    start_spread(sets[1])
-    start_spread(sets[0])
-    relay(sets[0])
-    relay(sets[1])
-    finish(sets[0])
+    second[5].start()
+    start_z(first[-1])
+    for one in first:
+        start_spread(one)
+    start_z(second)
+    for one in first:
+        relay(one)
+    start_spread(second)
+    relay(second)
+    finish(second)
     here = block(member, quarter)
     last = [copy(q2r, g2_ref.at[here], node, p) for p in peers]
     for one in last:
         one.start()
     g2_ref[here] = q2r[...]
-    finish(sets[1])
-    for one in up_copies + [to_partner_a, to_across, to_partner_b, pg_partner, pg_across, pg_forward]:
+    for one in first:
+        finish(one)
+    for one in up_copies + [to_partner_a, to_across, to_partner_b, pg_partner] + pg_across + pg_forward:
         one.wait_send()
     for one in g2_copies:
         one.wait_send()
@@ -467,17 +479,16 @@
         cols = stored.shape[1]
         total = vertex.shape[0]
         used = lax.broadcasted_iota(jnp.int32, neighbors.shape, 2) < counts[:, :, None]
-        masked = jnp.where(used, neighbors, -1)
+        masked = jnp.where(used, neighbors, 4 * rows)
         ids = jnp.concatenate(
             [masked[0], masked[1], vertex[:, None], counts[0][:, None], counts[1][:, None]], axis=1
         )
-        w1 = jnp.concatenate([self_w1, neigh_w1], axis=0)
-        w2 = jnp.concatenate([self_w2, neigh_w2], axis=0)
         scale = 1.0 / math.sqrt(total * mesh_node)
         depth = mesh_node // 2
         wide = 2 * cols
         quarter = 2 * width // 4
-        copies = 18 + 2 * (2 + 3 * (depth - 1))
+        groups = wide // quarter + 1
+        copies = 24 + groups * (2 + 3 * (depth - 1))
         vm = pltpu.VMEM
         scratch = [
             vm((rows, width), f32),
@@ -500,12 +511,9 @@
             vm((quarter, width), f32),
             vm((quarter, width), f32),
             vm((rows, width), f32),
-            vm((wide // 2, width), f32),
-            vm((wide // 2, width), f32),
-            vm((depth - 1, wide // 2 // depth, width), f32),
-            vm((quarter // 2, width), f32),
-            vm((quarter // 2, width), f32),
-            vm((depth - 1, quarter // 2 // depth, width), f32),
+            vm((groups, quarter // 2, width), f32),
+            vm((groups, quarter // 2, width), f32),
+            vm((groups, depth - 1, quarter // 2 // depth, width), f32),
             pltpu.SemaphoreType.DMA((copies,)),
             pltpu.SemaphoreType.DMA((copies,)),
         ]
@@ -517,13 +525,13 @@
                 jax.ShapeDtypeStruct((wide, width), f32),
                 jax.ShapeDtypeStruct((2 * width, width), f32),
             ),
-            in_specs=[space] * 5,
+            in_specs=[space] * 7,
             out_specs=(space,) * 3,
             scratch_shapes=scratch,
             compiler_params=pltpu.CompilerParams(
                 collective_id=0, has_side_effects=True, vmem_limit_bytes=60 * 1024 * 1024
             ),
-        )(stored, ids, w1, w2, upstream)
+        )(stored, ids, self_w1, neigh_w1, self_w2, neigh_w2, upstream)
         return out, g1[:cols], g1[cols:], g2[:width], g2[width:]
 
     return run
@@ -543,10 +551,11 @@
             and depth > 1
             and own * members * graphs == vertex.shape[0]
             and own % 64 == 0
+            and own * members <= 512
             and width % 128 == 0
             and stored.shape[1] % 128 == 0
             and (width // 4) % (8 * depth) == 0
-            and stored.shape[1] % (8 * depth) == 0
+            and (2 * stored.shape[1]) % (width // 2) == 0
         )
         return (fused(node_total) if fits else body)(*args)
 

time: 95.9 us -> 86.6 us (0.903)
  Pallas kernels: 85.2 us -> 77.9 us
  other arithmetic: 3.67 us -> 0.98 us
    pallas_call x1, Pallas kernels: 85.2 us -> 77.9 us  [run(): pl.pallas_call(functools.partial(fused_kernel, mesh_node, slots, scale),...]
    concatenate x2 -> x0, other arithmetic: 2.69 us -> none  [the longest x1 1.86 us: run(): w1 = jnp.concatenate([self_w1, neigh_w1], axis=0)]
where the time goes in v2:
time: 86.6 us; the launch traced here: 85.5 us
  Pallas kernels  77.9 us (90%)
  local copies, waits for them, and re-layouts  5.94 us (7%)
  other arithmetic  0.98 us (1%)
    pallas_call x1, Pallas kernels, run(): pl.pallas_call(functools.partial(fused_kernel, mesh_node, slots, scale),...  77.9 us
    slice x1, local copies, waits for them, and re-layouts, run(): return (out, g1[:cols], g1[cols:], g2[:width], g2[width:])  2.23 us
    concatenate x2, local copies, waits for them, and re-layouts, run(): jnp.concatenate([masked[0], masked[1], vertex[:, None], counts[0][:, None...  2.09 us

profile of v2, /device:TPU:0, one launch (start us, length us, event | category | flops | bytes accessed | tf_op | source)
XLA Modules:
  0.0 85.5 jit_solution(11297391867866505826)
XLA Ops:
  0.6 0.8 slice_bitcast_fusion.2
  1.4 1.0 %fusion = s32[2,2048,16]{1,2,0:T(8,128)S(1)} fusion(s32[2,2048,16]{1,2,0:T(8,128)} %param.11, s32[2,2048]{1,0:T(2,128)} %param.12), kind=kLoop, calls=%fused_computation.1 | loop fusion | flops 131072 | bytes 540672 | tf_op jit(solution)/shard_map/jit(_where)/select_n | solution.py:482
  2.5 0.8 concatenate.3
  3.2 1.3 %copy.19.ids_ref = s32[2048,35]{1,0:T(8,128)} copy(s32[2048,35]{0,1:T(8,128)S(1)} %concatenate.3) | data formatting | bytes 573440 | tf_op jit(solution)/shard_map/concatenate | solution.py:483
  4.5 77.9 %shard_map.128 = (f32[4,128,256]{2,1,0:T(8,128)}, f32[512,256]{1,0:T(8,128)}, f32[512,256]{1,0:T(8,128)}) custom-call(f32[2048,256]{1,0:T(8,128)} %store_ref.1, s32[2048,35]{1,0:T(8,128)} %copy.19.ids_ref, f32[256,256]{1,0:T(8,128)} %s1_ref.1, f32[256,256]{1,0:T(8,128)} %n1_ref.1, f32[256,256]{1,0:T(8,128)} %s2_ref.1, f32[256,256]{1,0:T(8,128)} %n2_ref.1, ...), custom_call_target="tpu_custom_call" | custom-call | tf_op jit(solution)/shard_map/pallas_call | solution.py:521
  82.4 0.0 copy-start
  82.4 2.2 %fusion.1 = (f32[256,256]{1,0:T(8,128)}, f32[256,256]{1,0:T(8,128)}, f32[256,256]{1,0:T(8,128)}, f32[256,256]{1,0:T(8,128)}) fusion(f32[512,256]{1,0:T(8,128)} %get-tuple-element.10, f32[512,256]{1,0:T(8,128)} %get-tuple-element.9), kind=kLoop, calls=%fused_computation.6 | loop fusion | bytes 2097152 | tf_op jit(solution)/shard_map/slice | solution.py:535
  84.7 0.0 copy-done
  84.7 0.8 copy.21
  (1 shorter events, 0.0 us)
Async XLA Ops:
  82.4 2.2 %copy-start = (f32[4,128,256]{2,1,0:T(8,128)S(1)}, f32[4,128,256]{2,1,0:T(8,128)}, u32[]{:S(2)}) copy-start(f32[4,128,256]{2,1,0:T(8,128)} %get-tuple-element.26) | copy-start | bytes 1572868

commit v3 on v2

--- a/solution.py
+++ b/solution.py
@@ -165,7 +165,9 @@
     slots,
     scale,
     store_ref,
-    ids_ref,
+    nbr_ref,
+    vertex_ref,
+    counts_ref,
     s1_ref,
     n1_ref,
     s2_ref,
@@ -185,6 +187,8 @@
     wh,
     wl,
     wt,
+    ids_t,
+    ids,
     onehot,
     adj,
     act_buf,
@@ -243,6 +247,7 @@
     def block(index, size):
         return pl.ds(pl.multiple_of(index * size, size), size)
 
+    ids_t[...] = jnp.zeros_like(ids_t)
     up_copies = [copy(up_ref.at[p], upg.at[block(member, own)], node, p) for p in peers]
     for one in up_copies:
         one.start()
@@ -261,20 +266,31 @@
             total = total + jnp.where(picked[:, k : k + 1] == lanes, one_b, none_b)
         return total
 
-    def build(graph, first, with_vertex):
+    def stage_ids(graph):
+        span = block(graph, rows)
+        slot = lax.broadcasted_iota(jnp.int32, (slots, rows), 0)
+        for layer in range(2):
+            used = slot < counts_ref[layer : layer + 1, span]
+            ids_t[layer * slots : (layer + 1) * slots] = jnp.where(
+                used, nbr_ref[layer, :, span], 4 * rows
+            )
+        ids_t[2 * slots : 2 * slots + 1] = vertex_ref[:, span]
+        ids_t[2 * slots + 1 : 2 * slots + 3] = counts_ref[:, span]
+        ids[...] = jnp.transpose(ids_t[...])
+
+    def build(first, with_vertex):
         @pl.loop(0, rows // tile)
         def _(t):
-            at = pl.ds(pl.multiple_of(graph * rows + t * tile, tile), tile)
-            picked = (ids_ref[at] - middle).astype(f32).astype(bf16)
+            picked = (ids[block(t, tile)] - middle).astype(f32).astype(bf16)
             to = block(t, tile)
             adj[to] = hits(picked, first)
             if with_vertex:
                 v = 2 * slots
                 onehot[to] = jnp.where(picked[:, v : v + 1] == lanes, one_b, none_b)
 
-    def reciprocal(graph, layer):
+    def reciprocal(layer):
         k = 2 * slots + 1 + layer
-        return 1.0 / ids_ref[block(graph, rows), k : k + 1].astype(f32)
+        return 1.0 / ids[:, k : k + 1].astype(f32)
 
     to_partner_a = copy(part.at[0], pin.at[0], node, partner)
     to_across = copy(part.at[1], far, node, across)
@@ -285,7 +301,8 @@
         gy = yc + (1 - s // 2) * (1 - 2 * yc)
         gc = cc + (1 - s % 2) * (1 - 2 * cc)
         graph = gy * 2 + gc
-        build(graph, 0, True)
+        stage_ids(graph)
+        build(0, True)
         sh, sl, st = thirds(store_ref[block(graph, rows)])
         fh = mul(onehot[...], sh).astype(bf16)
         fl = mul(onehot[...], sl).astype(bf16)
@@ -293,7 +310,7 @@
         xh[s, :, :cols] = fh
         xl[s, :, :cols] = fl
         xt[:, :cols] = ft
-        agg = (mul(adj[...], ft) + mul(adj[...], fl) + mul(adj[...], fh)) * reciprocal(graph, 0)
+        agg = (mul(adj[...], ft) + mul(adj[...], fl) + mul(adj[...], fh)) * reciprocal(0)
         ah, al, at = thirds(agg)
         xt[:, cols:] = at
         xh[s, :, cols:] = ah
@@ -314,8 +331,8 @@
         def _():
             to_partner_b.start()
 
-    build(member, slots, False)
-    shrink = reciprocal(member, 1)
+    build(slots, False)
+    shrink = reciprocal(1)
     for one in up_copies:
         one.wait_recv()
     scaled = halves(upg[...] * scale)
@@ -478,11 +495,7 @@
         slots = neighbors.shape[2]
         cols = stored.shape[1]
         total = vertex.shape[0]
-        used = lax.broadcasted_iota(jnp.int32, neighbors.shape, 2) < counts[:, :, None]
-        masked = jnp.where(used, neighbors, 4 * rows)
-        ids = jnp.concatenate(
-            [masked[0], masked[1], vertex[:, None], counts[0][:, None], counts[1][:, None]], axis=1
-        )
+        turned = jnp.transpose(neighbors, (0, 2, 1))
         scale = 1.0 / math.sqrt(total * mesh_node)
         depth = mesh_node // 2
         wide = 2 * cols
@@ -502,6 +515,8 @@
             vm((wide, width), bf16),
             vm((wide, width), bf16),
             vm((wide, width), bf16),
+            vm((128, rows), jnp.int32),
+            vm((rows, 128), jnp.int32),
             vm((rows, rows), bf16),
             vm((rows, rows), bf16),
             vm((rows, width), f32),
@@ -525,13 +540,13 @@
                 jax.ShapeDtypeStruct((wide, width), f32),
                 jax.ShapeDtypeStruct((2 * width, width), f32),
             ),
-            in_specs=[space] * 7,
+            in_specs=[space] * 9,
             out_specs=(space,) * 3,
             scratch_shapes=scratch,
             compiler_params=pltpu.CompilerParams(
                 collective_id=0, has_side_effects=True, vmem_limit_bytes=60 * 1024 * 1024
             ),
-        )(stored, ids, self_w1, neigh_w1, self_w2, neigh_w2, upstream)
+        )(stored, turned, vertex[None], counts, self_w1, neigh_w1, self_w2, neigh_w2, upstream)
         return out, g1[:cols], g1[cols:], g2[:width], g2[width:]
 
     return run
@@ -552,6 +567,8 @@
             and own * members * graphs == vertex.shape[0]
             and own % 64 == 0
             and own * members <= 512
+            and 2 * args[2].shape[2] + 3 <= 128
+            and args[2].shape[2] % 8 == 0
             and width % 128 == 0
             and stored.shape[1] % 128 == 0
             and (width // 4) % (8 * depth) == 0

time: 86.6 us -> 82.6 us (0.954)
  local copies, waits for them, and re-layouts: 5.94 us -> 3.02 us
  other arithmetic: 0.98 us -> 0 us
    concatenate x2 -> x0, local copies, waits for them, and re-layouts: 2.09 us -> none  [run(): jnp.concatenate([masked[0], masked[1], vertex[:, None], counts[0][:, None...]
    select_n x1 -> x0, other arithmetic: 0.98 us -> none  [run(): masked = jnp.where(used, neighbors, 4 * rows)]
where the time goes in v3:
time: 82.6 us; the launch traced here: 81.8 us
  Pallas kernels  78.1 us (95%)
  local copies, waits for them, and re-layouts  3.02 us (4%)
    pallas_call x1, Pallas kernels, run(): pl.pallas_call(functools.partial(fused_kernel, mesh_node, slots, scale),...  78.1 us
    slice x1, local copies, waits for them, and re-layouts, run(): return (out, g1[:cols], g1[cols:], g2[:width], g2[width:])  2.23 us

profile of v3, /device:TPU:0, one launch (start us, length us, event | category | flops | bytes accessed | tf_op | source)
XLA Modules:
  0.0 81.8 jit_solution(18165074086117014866)
XLA Ops:
  0.6 78.1 %shard_map.128 = (f32[4,128,256]{2,1,0:T(8,128)}, f32[512,256]{1,0:T(8,128)}, f32[512,256]{1,0:T(8,128)}) custom-call(f32[2048,256]{1,0:T(8,128)} %store_ref.1, s32[2,16,2048]{2,1,0:T(8,128)} %bitcast.2, s32[1,2048]{1,0:T(1,128)} %bitcast.3, s32[2,2048]{1,0:T(2,128)} %counts_ref.1, f32[256,256]{1,0:T(8,128)} %s1_ref.1, f32[256,256]{1,0:T(8,128)} %n1_ref.1, ...), custom_call_target="tpu_custom_call" | custom-call | tf_op jit(solution)/shard_map/pallas_call | solution.py:536
  78.8 0.0 copy-start
  78.8 2.2 %fusion = (f32[256,256]{1,0:T(8,128)}, f32[256,256]{1,0:T(8,128)}, f32[256,256]{1,0:T(8,128)}, f32[256,256]{1,0:T(8,128)}) fusion(f32[512,256]{1,0:T(8,128)} %get-tuple-element.10, f32[512,256]{1,0:T(8,128)} %get-tuple-element.9), kind=kLoop, calls=%fused_computation | loop fusion | bytes 2097152 | tf_op jit(solution)/shard_map/slice | solution.py:550
  81.0 0.0 copy-done
  81.0 0.8 copy.15
Async XLA Ops:
  78.8 2.2 %copy-start = (f32[4,128,256]{2,1,0:T(8,128)S(1)}, f32[4,128,256]{2,1,0:T(8,128)}, u32[]{:S(2)}) copy-start(f32[4,128,256]{2,1,0:T(8,128)} %get-tuple-element.22) | copy-start | bytes 1572868
